TPU v7x, 32 devices: a whole 2x2x4 slice. The times are simulated.
32 devices in a mesh: ctx: 8 (over z, y), grp: 2 (over core), head: 2 (over x).
Axes of the slice: x: 2, y: 2, z: 4, core: 2. Of those that a mesh axis runs over, the one named last changes fastest.
Arguments:
- residual: bfloat16 [2048, 2880], P(('ctx', 'grp')), may hold values from -10 to 10
- queries: bfloat16 [2048, 2048], P(('ctx', 'grp'), 'head'), may hold values from -32 to 32
- keys: bfloat16 [2048, 256], P(('ctx', 'grp'), 'head'), may hold values from -32 to 32
- values: bfloat16 [2048, 256], P(('ctx', 'grp'), 'head'), may hold values from -12 to 12
- out_weight: bfloat16 [2048, 2880], P('head'), may hold values from -0.125 to 0.125
- norm_gain: float32 [2880], replicated, may hold values from 0.5 to 1.5
- routes: int32 [2048, 4], P(('ctx', 'grp')), may hold values from 0 to 7, all different within a row; in each aligned block of 128 rows (0 to 127, 128 to 255, ...) at most 72 rows name the same one
- expert_weight: bfloat16 [8, 2880, 2, 1536], P('ctx', None, None, 'head'), may hold values from -0.109375 to 0.109375
Outputs:
- hidden: bfloat16 [2048, 2880], P(('ctx', 'grp'), 'head')
- active: bfloat16 [8, 2, 576, 1536], P('ctx', 'grp', None, 'head')
Inputs may be any that keep to these rules, and one draw needn't show every extreme that they name: `routes`: each token names 4 different experts; the 128 rows of one device name any one expert at most 72 times.
All inputs are finite; a program needn't handle non-finite values.
Results may differ from a plain program's by a relative error of at most 0.017.
Values may be sent and summed in bfloat16 or wider, within the bound.
A program may use at most 128 MiB of HBM per device.

v0:
```python
import jax
import jax.numpy as jnp
from jax import lax
from jax.sharding import PartitionSpec as P

D = 2880
HD = 64
TOP = 4


def shifted(value, axis, by):
    count = lax.axis_size(axis)
    pairs = [(i, i + by) for i in range(count) if 0 <= i + by < count]
    return lax.ppermute(value, axis, pairs)


def attend_block(running, query_heads, key_block, value_block, query_place, key_place, band):
    allowed = (
        (key_place[None, :] <= query_place[:, None])
        & (query_place[:, None] - key_place[None, :] < band)
        & (key_place[None, :] >= 0)
    )

    def attend_live(carried):
        row_max, row_total, summed = carried
        scores = jnp.einsum(
            "tkgd,skd->kgts", query_heads, key_block, preferred_element_type=jnp.float32
        )
        scores = jnp.where(allowed, scores * query_heads.shape[-1] ** (-0.5), -1e30)
        new_max = jnp.maximum(row_max, jnp.max(scores, axis=-1))
        weights = jnp.where(allowed, jnp.exp(scores - new_max[..., None]), 0.0)
        factor = jnp.exp(row_max - new_max)
        row_total = row_total * factor + jnp.sum(weights, axis=-1)
        summed = summed * factor[..., None] + jnp.einsum(
            "kgts,skd->kgtd",
            weights.astype(jnp.bfloat16),
            value_block,
            preferred_element_type=jnp.float32,
        )
        return (new_max, row_total, summed)

    def skip_block(carried):
        return carried

    return lax.cond(jnp.any(allowed), attend_live, skip_block, running)


def finish_rows(gate_up, squares, hidden_width):
    inverse_rms = lax.rsqrt(squares / D + 1e-05)
    gate_part = gate_up[..., :hidden_width] * inverse_rms[..., None]
    up_part = gate_up[..., hidden_width:] * inverse_rms[..., None]
    return (gate_part * jax.nn.sigmoid(1.702 * gate_part) * (up_part + 1.0)).astype(jnp.bfloat16)


def body(residual, queries, keys, values, out_weight, norm_gain, routes, expert_weight):
    tokens_here = queries.shape[0]
    kv_local = keys.shape[1] // HD
    per_group = queries.shape[1] // keys.shape[1]
    query_heads = queries.reshape(tokens_here, kv_local, per_group, HD)
    ctx_index = lax.axis_index("ctx")
    grp_index = lax.axis_index("grp")
    head_index = lax.axis_index("head")
    heads_count = lax.axis_size("head")
    block_len = tokens_here * lax.axis_size("grp")
    reach_steps = max(1, lax.axis_size("ctx") // 16)
    band = reach_steps * block_len
    query_place = (
        ctx_index * block_len + grp_index * tokens_here + jnp.arange(tokens_here, dtype=jnp.int32)
    )
    own_keys, own_values = (
        lax.all_gather(keys, "grp", axis=0, tiled=True),
        lax.all_gather(values, "grp", axis=0, tiled=True),
    )

    def attend_from(running, key_flat, value_flat, distance):
        key_place = (ctx_index - distance) * block_len + jnp.arange(block_len, dtype=jnp.int32)
        return attend_block(
            running,
            query_heads,
            key_flat.reshape(block_len, kv_local, HD),
            value_flat.reshape(block_len, kv_local, HD),
            query_place,
            key_place,
            band,
        )

    running = (
        jnp.full((kv_local, per_group, tokens_here), -1e30, jnp.float32),
        jnp.zeros((kv_local, per_group, tokens_here), jnp.float32),
        jnp.zeros((kv_local, per_group, tokens_here, HD), jnp.float32),
    )
    running = attend_from(running, own_keys, own_values, 0)

    def cycle_turn(distance, carried):
        running, key_flat, value_flat = carried
        key_flat, value_flat = shifted((key_flat, value_flat), "ctx", 1)
        running = attend_from(running, key_flat, value_flat, distance)
        return (running, key_flat, value_flat)

    running = lax.fori_loop(1, reach_steps + 1, cycle_turn, (running, own_keys, own_values))[0]
    row_max, row_total, summed = running
    mixed = summed / row_total[..., None]
    attended = (
        jnp.transpose(mixed, (2, 0, 1, 3))
        .reshape(tokens_here, kv_local * per_group * HD)
        .astype(jnp.bfloat16)
    )
    partial_value = jnp.dot(attended, out_weight, preferred_element_type=jnp.float32)
    column_width = D // heads_count
    experts_all = expert_weight.shape[0] * lax.axis_size("ctx")
    routed = tokens_here * TOP
    capacity = min(tokens_here, routed // experts_all + max(1, routed // (8 * experts_all)))
    flat_routes = routes.reshape(routed)
    expert_hits = (
        flat_routes[:, None] == jnp.arange(experts_all, dtype=jnp.int32)[None, :]
    ).astype(jnp.bfloat16)
    earlier = jnp.tril(jnp.ones((routed, routed), jnp.bfloat16), -1)
    before = jnp.dot(earlier, expert_hits, preferred_element_type=jnp.float32)
    slot_index = jnp.sum(before * expert_hits.astype(jnp.float32), axis=1).astype(jnp.int32)
    hidden_width = expert_weight.shape[3]
    local_weight = expert_weight[0].reshape(D, 2 * hidden_width)
    projected = lax.psum_scatter(
        partial_value.astype(jnp.bfloat16), "head", scatter_dimension=1, tiled=True
    ).astype(jnp.float32)
    own_residual = lax.dynamic_slice_in_dim(residual, head_index * column_width, column_width, 1)
    hidden = (own_residual.astype(jnp.float32) + projected).astype(jnp.bfloat16)
    dest_index = flat_routes * capacity + slot_index
    route_rows = jnp.repeat(hidden, TOP, axis=0)
    outgoing = (
        jnp.zeros((experts_all * capacity, column_width), jnp.bfloat16)
        .at[dest_index]
        .set(route_rows)
    )
    arrived = lax.all_to_all(
        outgoing.reshape(experts_all, capacity, column_width),
        "ctx",
        split_axis=0,
        concat_axis=1,
        tiled=True,
    )
    arrived_rows = arrived.reshape(-1, column_width)
    slot_total = arrived_rows.shape[0]
    widened = lax.all_gather(arrived_rows, "head", axis=1, tiled=True).astype(jnp.float32)
    scaled = (widened * norm_gain[None, :]).astype(jnp.bfloat16)
    gate_up = jnp.dot(scaled, local_weight, preferred_element_type=jnp.float32)
    squares = jnp.sum(widened * widened, axis=1)
    gate_up, squares = (gate_up, squares)
    active = finish_rows(gate_up, squares, hidden_width)
    return (hidden, active.reshape(1, 1, slot_total, hidden_width))


def solution(mesh):
    in_specs = (
        P(("ctx", "grp"), None),
        P(("ctx", "grp"), "head"),
        P(("ctx", "grp"), "head"),
        P(("ctx", "grp"), "head"),
        P("head", None),
        P(),
        P(("ctx", "grp"), None),
        P("ctx", None, None, "head"),
    )
    out_specs = (P(("ctx", "grp"), "head"), P("ctx", "grp", None, "head"))
    return jax.shard_map(body, mesh=mesh, in_specs=in_specs, out_specs=out_specs, check_vma=False)
```

profile of v0, /device:TPU:8, one launch (start us, length us, event | category | flops | bytes accessed | tf_op | source)
XLA Modules:
  0.0 195.2 jit_solution(11392658521346276499)
XLA Ops:
  8.1 2.0 %all_gather.9 = bf16[256,128]{0,1:T(8,128)(2,1)} all-gather(bf16[128,128]{0,1:T(8,128)(2,1)S(1)} %copy.35), channel_id=1, replica_groups=mesh['ctx'=8,'grp'=2,'head'=2] {'grp'}, dimensions={0}, use_global_device_ids=true | all-gather | bytes 98304 | tf_op jit(solution)/shard_map/all_gather | solution.py:71
  10.1 3.4 %collective-permute-start = (bf16[256,128]{0,1:T(8,128)(2,1)}, bf16[256,128]{0,1:T(8,128)(2,1)S(1)}, u32[]{:S(2)}, u32[]{:S(2)}) collective-permute-start(bf16[256,128]{0,1:T(8,128)(2,1)} %all_gather.9), channel_id=1, source_target_pairs={{0,4},{4,8},{8,12},{12,16},{16,20},{20,24},{24,28},{1,5},{5,9},{9,... | collective-permute-start | bytes 196616 | tf_op jit(solution)/shard_map/while/body/eval_jaxpr/ppermute | solution.py:14
  13.5 0.9 copy.37
  14.4 2.0 %all_gather.10 = bf16[256,128]{0,1:T(8,128)(2,1)} all-gather(bf16[128,128]{0,1:T(8,128)(2,1)S(1)} %copy.37), channel_id=1, replica_groups=mesh['ctx'=8,'grp'=2,'head'=2] {'grp'}, dimensions={0}, use_global_device_ids=true | all-gather | bytes 98304 | tf_op jit(solution)/shard_map/all_gather | solution.py:72
  16.4 3.4 %collective-permute-start.1 = (bf16[256,128]{0,1:T(8,128)(2,1)}, bf16[256,128]{0,1:T(8,128)(2,1)S(1)}, u32[]{:S(2)}, u32[]{:S(2)}) collective-permute-start(bf16[256,128]{0,1:T(8,128)(2,1)} %all_gather.10), channel_id=1, source_target_pairs={{0,4},{4,8},{8,12},{12,16},{16,20},{20,24},{24,28},{1,5},{5,9},{9,... | collective-permute-start | bytes 196616 | tf_op jit(solution)/shard_map/while/body/eval_jaxpr/ppermute | solution.py:14
  20.7 1.1 copy.36
  23.1 5.3 %conditional.2 = (f32[2,8,128]{2,1,0:T(8,128)}, f32[2,8,128]{2,1,0:T(8,128)S(1)}, f32[2,8,128,64]{2,3,1,0:T(8,128)S(1)}) conditional(s32[]{:T(128)} %convert_element_type.65, () %tuple.30, (pred[128,256]{0,1:T(8,128)(4,1)S(1)}, bf16[256,128]{0,1:T(8,128)(2,1)}, bf16[128,2,8,64]{0,3,2,1:T(8,128)(2,1)S(1)}, bf16[256,128]{0,1:T(8,128)(2,1)}) %tuple.54), branch_computations={%region_2.3_spmd, %region_3.6_spmd} | conditional | flops 141172736 | bytes 7397400 | solution.py:45
  23.2 1.3 fusion
  25.1 1.4 convolution_add_fusion
  26.5 1.2 fusion.2
  28.5 3.1 %conditional.3 = ((f32[2,8,128]{2,1,0:T(8,128)S(1)}, f32[2,8,128,64]{2,3,1,0:T(8,128)S(1)})) conditional(s32[]{:T(128)} %convert_element_type.64, (f32[2,8,128]{2,1,0:T(8,128)S(1)}, f32[2,8,128,64]{2,3,1,0:T(8,128)S(1)}) %tuple.32, (pred[128,256]{0,1:T(8,128)(4,1)S(1)}, bf16[256,128]{0,1:T(8,128)(2,1)S(1)}, bf16[128,2,8,64]{0,3,2,1:T(8,128)(2,1)S(1)}, ...), branch_computations={%region_6.0_spmd, %region_7.10_spmd} | conditional | flops 141299712 | bytes 7946264 | solution.py:45
  31.6 5.2 %convolution_convert_fusion = bf16[128,2880]{0,1:T(8,128)(2,1)} fusion(bf16[1024,2880]{0,1:T(8,128)(2,1)} %param.16, bf16[128,1024]{0,1:T(8,128)(2,1)S(1)} %bitcast.76), kind=kOutput, calls=%fused_computation.34 | convolution fusion | flops 755343360 | bytes 6897664 | tf_op jit(solution)/shard_map/dot_general | solution.py:108
  37.8 16.4 %reduce-scatter.2.cloned.1.call-done = bf16[128,1440]{0,1:T(8,128)(2,1)} async-done(((bf16[128,2880]{0,1:T(8,128)(2,1)}), bf16[128,1440]{0,1:T(8,128)(2,1)}) %reduce-scatter.2.cloned.1.call-update) | async-done | bytes 368656 | tf_op jit(solution)/shard_map/reduce_scatter | solution.py:122
  54.2 1.1 add_convert_fusion
  57.4 3.5 %scatter_custom_fusion = bf16[576,1440]{1,0:T(8,128)(2,1)S(1)} fusion(s32[512]{0:T(512)S(1)} %bitcast.79, bf16[512,1440]{1,0:T(8,128)(2,1)S(1)} %reshape.122, bf16[]{:T(256)} %constant.49.clone.1), kind=kCustom, calls=%fused_computation.46 | custom fusion | bytes 1658882 | tf_op jit(solution)/shard_map/scatter | solution.py:132
  60.9 46.2 %all_to_all.4 = bf16[8,72,1440]{2,1,0:T(8,128)(2,1)} all-to-all(bf16[8,72,1440]{2,1,0:T(8,128)(2,1)S(1)} %bitcast.73), channel_id=1, replica_groups=mesh['ctx'=8,'grp'=2,'head'=2] {'ctx'}, dimensions={0} | all-to-all | bytes 3317760 | tf_op jit(solution)/shard_map/all_to_all | solution.py:134
  107.1 9.0 %copy.48 = bf16[360,8,2,768]{3,1,2,0:T(8,128)(2,1)} copy(bf16[360,8,2,768]{3,2,1,0:T(2,128)(2,1)} %bitcast.70) | data formatting | bytes 17694720
  116.1 38.8 %all-gather.3.cloned.1.call-done = bf16[2,1440,576]{1,2,0:T(8,128)(2,1)} async-done(((bf16[1,1440,576]{1,2,0:T(8,128)(2,1)}), bf16[2,1440,576]{1,2,0:T(8,128)(2,1)}) %all-gather.3.cloned.1.call-update) | async-done | bytes 3317776 | tf_op jit(solution)/shard_map/all_gather | solution.py:143
  155.0 8.6 %copy.41 = f32[2,1440,576]{1,0,2:T(2,128)} copy(bf16[2,1440,576]{1,2,0:T(8,128)(2,1)} %all-gather.3.cloned.1.call-done) | data formatting | bytes 9953280 | tf_op jit(solution)/shard_map/convert_element_type | solution.py:143
  163.5 10.2 %reshape.128 = f32[2880,576]{0,1:T(8,128)} reshape(f32[2,1440,576]{1,0,2:T(2,128)} %copy.41) | data formatting | bytes 13271040 | tf_op jit(solution)/shard_map/convert_element_type | solution.py:143
  173.7 3.6 %multiply_reduce_fusion = f32[576]{0:T(1024)S(1)} fusion(f32[2880,576]{0,1:T(8,128)} %reshape.128), kind=kLoop, calls=%fused_computation.32 | loop fusion | flops 3317184 | bytes 6637824 | tf_op jit(solution)/shard_map/reduce_sum | solution.py:146
  177.4 1.2 copy-done
  178.6 8.2 %fusion.23 = f32[576,1536]{1,0:T(8,128)S(1)} fusion(bf16[2880,1536]{1,0:T(8,128)(2,1)} %bitcast.71, f32[2880,576]{0,1:T(8,128)S(1)} %copy-done, f32[2880]{0:T(1024)S(1)} %copy-done.4), kind=kOutput, calls=%fused_computation.35 | convolution fusion | flops 5099397120 | bytes 19033344 | tf_op jit(solution)/shard_map/dot_general | solution.py:145
  186.8 1.6 fusion.32
  (41 shorter events, 9.2 us)
Async XLA Ops:
  7.2 47.0 %reduce-scatter.2.cloned.1.call-start = ((), (), s32[]{:S(2)}) async-start(), calls=%async_computation.2 | async-start | bytes 1105920 | tf_op jit(solution)/shard_map/reduce_scatter | solution.py:122
  10.1 18.4 %collective-permute-start = (bf16[256,128]{0,1:T(8,128)(2,1)}, bf16[256,128]{0,1:T(8,128)(2,1)S(1)}, u32[]{:S(2)}, u32[]{:S(2)}) collective-permute-start(bf16[256,128]{0,1:T(8,128)(2,1)} %all_gather.9), channel_id=1, source_target_pairs={{0,4},{4,8},{8,12},{12,16},{16,20},{20,24},{24,28},{1,5},{5,9},{9,... | collective-permute-start | bytes 196616 | tf_op jit(solution)/shard_map/while/body/eval_jaxpr/ppermute | solution.py:14
  16.4 12.1 %collective-permute-start.1 = (bf16[256,128]{0,1:T(8,128)(2,1)}, bf16[256,128]{0,1:T(8,128)(2,1)S(1)}, u32[]{:S(2)}, u32[]{:S(2)}) collective-permute-start(bf16[256,128]{0,1:T(8,128)(2,1)} %all_gather.10), channel_id=1, source_target_pairs={{0,4},{4,8},{8,12},{12,16},{16,20},{20,24},{24,28},{1,5},{5,9},{9,... | collective-permute-start | bytes 196616 | tf_op jit(solution)/shard_map/while/body/eval_jaxpr/ppermute | solution.py:14
  31.6 5.3 %copy-start.3 = (s32[128,4]{0,1:T(4,128)S(1)}, s32[128,4]{0,1:T(4,128)}, u32[]{:S(2)}) copy-start(s32[128,4]{0,1:T(4,128)} %param.18) | copy-start | bytes 6148
  36.9 17.3 %copy-start.2 = (bf16[128,2880]{0,1:T(8,128)(2,1)S(1)}, bf16[128,2880]{0,1:T(8,128)(2,1)}, u32[]{:S(2)}) copy-start(bf16[128,2880]{0,1:T(8,128)(2,1)} %param.12) | copy-start | bytes 2211844
  36.9 118.1 %all-gather.3.cloned.1.call-start = ((), (), s32[]{:S(2)}) async-start(), calls=%async_computation.3 | async-start | bytes 5308416 | tf_op jit(solution)/shard_map/all_gather | solution.py:143
  55.3 0.7 copy-start.1
  173.7 4.9 %copy-start = (f32[2880,576]{0,1:T(8,128)S(1)}, f32[2880,576]{0,1:T(8,128)}, u32[]{:S(2)}) copy-start(f32[2880,576]{0,1:T(8,128)} %reshape.128) | copy-start | bytes 19906564
  173.7 4.9 %copy-start.4 = (f32[2880]{0:T(1024)S(1)}, f32[2880]{0:T(1024)}, u32[]{:S(2)}) copy-start(f32[2880]{0:T(1024)} %param.17) | copy-start | bytes 34564
Sparse Core Ops, SparseCore 0:
  37.0 17.0 reduce-scatter.1
  107.2 47.6 all-gather.2
where the time goes:
time: 198 us; the launch traced here: 195 us
  waiting for transfers between devices  55.2 us (28%)
  blocking collectives  50.2 us (25%)
  local copies, waits for them, and re-layouts  37.9 us (19%)
  matrix products  17.7 us (9%)
  between operations  15.6 us (8%)
  other arithmetic  11.7 us (6%)
  starting transfers between devices  6.91 us (3%)
    all_to_all x1, blocking collectives, body(): lax.all_to_all(outgoing.reshape(experts_all, capacity, column_width), 'ct...  46.2 us
    all_gather x1, waiting for transfers between devices, body(): lax.all_gather(arrived_rows, 'head', axis=1, tiled=True).astype(jnp.float32)  38.8 us
    convert_element_type x2, local copies, waits for them, and re-layouts, body(): lax.all_gather(arrived_rows, 'head', axis=1, tiled=True).astype(jnp.float32)  18.8 us
    reduce_scatter x1, waiting for transfers between devices, body(): lax.psum_scatter(partial_value.astype(jnp.bfloat16), 'head', scatter_dime...  16.4 us
    unnamed x15, local copies, waits for them, and re-layouts  14 us
    dot_general x1, matrix products, body(): gate_up = jnp.dot(scaled, local_weight, preferred_element_type=jnp.float32)  8.21 us
    ppermute x2, starting transfers between devices, shifted(): return lax.ppermute(value, axis, pairs)  6.83 us
    dot_general x1, matrix products, body(): jnp.dot(attended, out_weight, preferred_element_type=jnp.float32)  5.25 us
  transfers between devices with their start and end apart: 4, of which 2 were waited for; matrix products, arithmetic and copies ran while one was open for 9% of the time, Pallas kernels for 0%

commit v1 on v0

--- a/solution.py
+++ b/solution.py
@@ -1,6 +1,9 @@
+import functools
 import jax
 import jax.numpy as jnp
 from jax import lax
+from jax.experimental import pallas as pl
+from jax.experimental.pallas import tpu as pltpu
 from jax.sharding import PartitionSpec as P
 
 D = 2880
@@ -45,11 +48,231 @@
     return lax.cond(jnp.any(allowed), attend_live, skip_block, running)
 
 
-def finish_rows(gate_up, squares, hidden_width):
-    inverse_rms = lax.rsqrt(squares / D + 1e-05)
-    gate_part = gate_up[..., :hidden_width] * inverse_rms[..., None]
-    up_part = gate_up[..., hidden_width:] * inverse_rms[..., None]
-    return (gate_part * jax.nn.sigmoid(1.702 * gate_part) * (up_part + 1.0)).astype(jnp.bfloat16)
+MESH = pl.DeviceIdType.MESH
+F32 = jnp.float32
+BF16 = jnp.bfloat16
+
+
+def turn_of(step, count):
+    return 1 + lax.rem(step + count // 2 - 1, count - 1)
+
+
+def layer_kernel(
+    count,
+    cap,
+    att_ref,
+    res_ref,
+    routes_ref,
+    gain_ref,
+    ow_hbm,
+    w_hbm,
+    hid_ref,
+    act_ref,
+    ow,
+    w,
+    psend,
+    precv,
+    hits_ref,
+    before_ref,
+    sbuf,
+    rbuf,
+    ow_sem,
+    w_sem,
+    psend_sem,
+    precv_sem,
+    send_sem,
+    recv_sem,
+    xsend_sem,
+    xrecv_sem,
+):
+    me = lax.axis_index("ctx")
+    head = lax.axis_index("head")
+    heads = rbuf.shape[0]
+    others = [lax.rem(head + j, heads) for j in range(1, heads)]
+    half, tokens = hid_ref.shape
+    width = act_ref.shape[2]
+
+    def ow_copy(which, slot):
+        rows = pl.ds(pl.multiple_of(which * half, 16), half)
+        return pltpu.make_async_copy(ow_hbm.at[rows], ow.at[slot], ow_sem.at[slot])
+
+    for j in range(1, heads):
+        ow_copy(others[j - 1], j).start()
+    ow_copy(head, 0).start()
+    pltpu.make_async_copy(w_hbm, w, w_sem).start()
+
+    barrier = pltpu.get_barrier_semaphore()
+    for other in others:
+        pl.semaphore_signal(barrier, inc=1, device_id={"head": other}, device_id_type=MESH)
+
+    def greet(step, carry):
+        peer = lax.rem(me + step, count)
+        pl.semaphore_signal(barrier, inc=1, device_id={"ctx": peer}, device_id_type=MESH)
+        return carry
+
+    lax.fori_loop(1, count, greet, 0)
+
+    def project(slot):
+        return lax.dot_general(
+            ow[slot], att_ref[...], (((1,), (1,)), ((), ())), preferred_element_type=F32
+        ).astype(BF16)
+
+    def exchange(j):
+        return pltpu.make_async_remote_copy(
+            src_ref=psend.at[j - 1],
+            dst_ref=precv.at[j - 1],
+            send_sem=psend_sem.at[j - 1],
+            recv_sem=precv_sem.at[j - 1],
+            device_id={"head": others[j - 1]},
+            device_id_type=MESH,
+        )
+
+    for j in range(1, heads):
+        ow_copy(others[j - 1], j).wait()
+        psend[j - 1] = project(j)
+        if j == 1:
+            pl.semaphore_wait(barrier, count - 1 + heads - 1)
+        exchange(j).start()
+    ow_copy(head, 0).wait()
+    projected = project(0).astype(F32)
+
+    expert_ids = lax.broadcasted_iota(jnp.int32, (count, tokens), 0)
+    hits = jnp.zeros((count, tokens), F32)
+    for k in range(routes_ref.shape[0]):
+        hits = hits + jnp.where(routes_ref[k : k + 1, :] == expert_ids, 1.0, 0.0)
+    earlier = jnp.where(
+        lax.broadcasted_iota(jnp.int32, (tokens, tokens), 0)
+        < lax.broadcasted_iota(jnp.int32, (tokens, tokens), 1),
+        1.0,
+        0.0,
+    ).astype(BF16)
+    hits_ref[...] = hits
+    before_ref[...] = jnp.dot(hits.astype(BF16), earlier, preferred_element_type=F32)
+    residual = res_ref[pl.ds(pl.multiple_of(head * half, 16), half), :].astype(F32)
+
+    for j in range(1, heads):
+        exchange(j).wait()
+        projected = projected + precv[j - 1].astype(F32)
+    hid_ref[...] = (residual + projected).astype(BF16)
+
+    slots = lax.broadcasted_iota(jnp.int32, (cap, tokens), 0).astype(F32)
+
+    def rows_for(expert):
+        wanted = hits_ref[pl.ds(expert, 1), :] > 0.5
+        picks = jnp.where((slots == before_ref[pl.ds(expert, 1), :]) & wanted, 1.0, 0.0)
+        return lax.dot_general(
+            picks.astype(BF16),
+            hid_ref[...],
+            (((1,), (1,)), ((), ())),
+            preferred_element_type=F32,
+        ).astype(BF16)
+
+    def routed(step):
+        turn = turn_of(step, count)
+        return pltpu.make_async_remote_copy(
+            src_ref=sbuf.at[turn],
+            dst_ref=rbuf.at[head, me],
+            send_sem=send_sem.at[turn],
+            recv_sem=recv_sem.at[me],
+            device_id={"ctx": lax.rem(me + turn, count)},
+            device_id_type=MESH,
+        )
+
+    def landed(source):
+        return pltpu.make_async_remote_copy(
+            src_ref=rbuf.at[head, source],
+            dst_ref=rbuf.at[head, source],
+            send_sem=send_sem.at[0],
+            recv_sem=recv_sem.at[source],
+            device_id={"head": others[0]},
+            device_id_type=MESH,
+        )
+
+    def crossed(j, source):
+        return pltpu.make_async_remote_copy(
+            src_ref=rbuf.at[head, source],
+            dst_ref=rbuf.at[head, source],
+            send_sem=xsend_sem.at[j - 1, source],
+            recv_sem=xrecv_sem.at[j - 1, source],
+            device_id={"head": others[j - 1]},
+            device_id_type=MESH,
+        )
+
+    def cross(source):
+        for j in range(1, heads):
+            crossed(j, source).start()
+
+    def mirror(source):
+        for j in range(1, heads):
+            origin = lax.rem(head + heads - j, heads)
+            pltpu.make_async_remote_copy(
+                src_ref=rbuf.at[origin, source],
+                dst_ref=rbuf.at[origin, source],
+                send_sem=xsend_sem.at[j - 1, source],
+                recv_sem=xrecv_sem.at[j - 1, source],
+                device_id={"head": others[j - 1]},
+                device_id_type=MESH,
+            ).wait_recv()
+
+    def dispatch(step, carry):
+        turn = turn_of(step, count)
+        sbuf[turn] = rows_for(lax.rem(me + turn, count))
+        routed(step).start()
+        return carry
+
+    lax.fori_loop(0, count - 1, dispatch, 0)
+    rbuf[head, me] = rows_for(me)
+    cross(me)
+    pltpu.make_async_copy(w_hbm, w, w_sem).wait()
+
+    def expert(source):
+        squares = jnp.zeros((cap, 1), F32)
+        parts = []
+        for part in range(heads):
+            rows = rbuf[part, source].astype(F32)
+            squares = squares + jnp.sum(rows * rows, axis=1, keepdims=True)
+            parts.append((rows * gain_ref[part : part + 1, :]).astype(BF16))
+        inverse_rms = lax.rsqrt(squares / (heads * half) + 1e-05)
+
+        def product(low):
+            total = jnp.zeros((cap, width), F32)
+            for part in range(heads):
+                total = total + jnp.dot(
+                    parts[part],
+                    w[part * half : (part + 1) * half, low : low + width],
+                    preferred_element_type=F32,
+                )
+            return total
+
+        gate = product(0) * inverse_rms
+        up = product(width) * inverse_rms
+        act_ref[source] = (gate * jax.nn.sigmoid(1.702 * gate) * (up + 1.0)).astype(BF16)
+
+    def receive(step, carry):
+        source = lax.rem(me + count - turn_of(step, count), count)
+        landed(source).wait_recv()
+        cross(source)
+        before = jnp.where(
+            step == 0, me, lax.rem(me + count - turn_of(jnp.maximum(step - 1, 0), count), count)
+        )
+        mirror(before)
+        expert(before)
+        return carry
+
+    lax.fori_loop(0, count - 1, receive, 0)
+    last = lax.rem(me + count - turn_of(count - 2, count), count)
+    mirror(last)
+    expert(last)
+
+    def drain(step, carry):
+        routed(step).wait_send()
+        for j in range(1, heads):
+            crossed(j, lax.rem(me + step + 1, count)).wait_send()
+        return carry
+
+    lax.fori_loop(0, count - 1, drain, 0)
+    for j in range(1, heads):
+        crossed(j, me).wait_send()
 
 
 def body(residual, queries, keys, values, out_weight, norm_gain, routes, expert_weight):
@@ -105,48 +328,53 @@
         .reshape(tokens_here, kv_local * per_group * HD)
         .astype(jnp.bfloat16)
     )
-    partial_value = jnp.dot(attended, out_weight, preferred_element_type=jnp.float32)
-    column_width = D // heads_count
-    experts_all = expert_weight.shape[0] * lax.axis_size("ctx")
+    width_all = residual.shape[1]
+    half = width_all // heads_count
+    count = lax.axis_size("ctx")
+    experts_all = expert_weight.shape[0] * count
     routed = tokens_here * TOP
-    capacity = min(tokens_here, routed // experts_all + max(1, routed // (8 * experts_all)))
-    flat_routes = routes.reshape(routed)
-    expert_hits = (
-        flat_routes[:, None] == jnp.arange(experts_all, dtype=jnp.int32)[None, :]
-    ).astype(jnp.bfloat16)
-    earlier = jnp.tril(jnp.ones((routed, routed), jnp.bfloat16), -1)
-    before = jnp.dot(earlier, expert_hits, preferred_element_type=jnp.float32)
-    slot_index = jnp.sum(before * expert_hits.astype(jnp.float32), axis=1).astype(jnp.int32)
+    cap = min(tokens_here, routed // experts_all + max(1, routed // (8 * experts_all)))
     hidden_width = expert_weight.shape[3]
-    local_weight = expert_weight[0].reshape(D, 2 * hidden_width)
-    projected = lax.psum_scatter(
-        partial_value.astype(jnp.bfloat16), "head", scatter_dimension=1, tiled=True
-    ).astype(jnp.float32)
-    own_residual = lax.dynamic_slice_in_dim(residual, head_index * column_width, column_width, 1)
-    hidden = (own_residual.astype(jnp.float32) + projected).astype(jnp.bfloat16)
-    dest_index = flat_routes * capacity + slot_index
-    route_rows = jnp.repeat(hidden, TOP, axis=0)
-    outgoing = (
-        jnp.zeros((experts_all * capacity, column_width), jnp.bfloat16)
-        .at[dest_index]
-        .set(route_rows)
-    )
-    arrived = lax.all_to_all(
-        outgoing.reshape(experts_all, capacity, column_width),
-        "ctx",
-        split_axis=0,
-        concat_axis=1,
-        tiled=True,
-    )
-    arrived_rows = arrived.reshape(-1, column_width)
-    slot_total = arrived_rows.shape[0]
-    widened = lax.all_gather(arrived_rows, "head", axis=1, tiled=True).astype(jnp.float32)
-    scaled = (widened * norm_gain[None, :]).astype(jnp.bfloat16)
-    gate_up = jnp.dot(scaled, local_weight, preferred_element_type=jnp.float32)
-    squares = jnp.sum(widened * widened, axis=1)
-    gate_up, squares = (gate_up, squares)
-    active = finish_rows(gate_up, squares, hidden_width)
-    return (hidden, active.reshape(1, 1, slot_total, hidden_width))
+    in_vmem = pl.BlockSpec(memory_space=pltpu.VMEM)
+    in_hbm = pl.BlockSpec(memory_space=pl.ANY)
+    hidden, active = pl.pallas_call(
+        functools.partial(layer_kernel, count, cap),
+        out_shape=(
+            jax.ShapeDtypeStruct((half, tokens_here), BF16),
+            jax.ShapeDtypeStruct((count, cap, hidden_width), BF16),
+        ),
+        in_specs=[in_vmem] * 4 + [in_hbm] * 2,
+        out_specs=(in_vmem, in_vmem),
+        scratch_shapes=[
+            pltpu.VMEM((heads_count, half, out_weight.shape[0]), BF16),
+            pltpu.VMEM((width_all, 2 * hidden_width), BF16),
+            pltpu.VMEM((heads_count - 1, half, tokens_here), BF16),
+            pltpu.VMEM((heads_count - 1, half, tokens_here), BF16),
+            pltpu.VMEM((count, tokens_here), F32),
+            pltpu.VMEM((count, tokens_here), F32),
+            pltpu.VMEM((count, cap, half), BF16),
+            pltpu.VMEM((heads_count, count, cap, half), BF16),
+            pltpu.SemaphoreType.DMA((heads_count,)),
+            pltpu.SemaphoreType.DMA,
+            pltpu.SemaphoreType.DMA((heads_count - 1,)),
+            pltpu.SemaphoreType.DMA((heads_count - 1,)),
+            pltpu.SemaphoreType.DMA((count,)),
+            pltpu.SemaphoreType.DMA((count,)),
+            pltpu.SemaphoreType.DMA((heads_count - 1, count)),
+            pltpu.SemaphoreType.DMA((heads_count - 1, count)),
+        ],
+        compiler_params=pltpu.CompilerParams(
+            collective_id=0, has_side_effects=True, vmem_limit_bytes=60 * 1024 * 1024
+        ),
+    )(
+        attended,
+        residual.T,
+        routes.T,
+        norm_gain.reshape(heads_count, half),
+        out_weight.T,
+        expert_weight[0].reshape(width_all, 2 * hidden_width),
+    )
+    return (hidden.T, active.reshape(1, 1, count * cap, hidden_width))
 
 
 def solution(mesh):

time: 198 us -> 121 us (0.61); the launches traced: 195 us -> 121 us
  Pallas kernels: 0 us -> 80.9 us
  waiting for transfers between devices: 55.2 us -> 0.01 us
  blocking collectives: 50.2 us -> 4.03 us
  local copies, waits for them, and re-layouts: 37.9 us -> 17.4 us
  matrix products: 17.7 us -> 3.9 us
  between operations: 15.6 us -> 2.08 us
  other arithmetic: 11.7 us -> 5.42 us
    pallas_call x0 -> x1, Pallas kernels: none -> 80.9 us  [body(): pl.pallas_call(functools.partial(layer_kernel, count, cap), out_shape=(ja...]
    all_to_all x1 -> x0, blocking collectives: 46.2 us -> none  [body(): lax.all_to_all(outgoing.reshape(experts_all, capacity, column_width), 'ct...]
    all_gather x1 -> x0, waiting for transfers between devices: 38.8 us -> none  [body(): lax.all_gather(arrived_rows, 'head', axis=1, tiled=True).astype(jnp.float32)]
    convert_element_type x3 -> x1, local copies, waits for them, and re-layouts: 18.9 us -> 0.85 us  [body(): attended = jnp.transpose(mixed, (2, 0, 1, 3)).reshape(tokens_here, kv_loc...]
    reduce_scatter x1 -> x0, waiting for transfers between devices: 16.4 us -> none  [body(): lax.psum_scatter(partial_value.astype(jnp.bfloat16), 'head', scatter_dime...]
    dot_general x3 -> x0, matrix products: 13.8 us -> none  [the longest x1 8.21 us: body(): gate_up = jnp.dot(scaled, local_weight, preferred_element_type=jnp.float32)]
    reduce_sum x1 -> x0, other arithmetic: 3.61 us -> none  [body(): squares = jnp.sum(widened * widened, axis=1)]
    scatter x1 -> x0, local copies, waits for them, and re-layouts: 3.5 us -> none  [body(): outgoing = jnp.zeros((experts_all * capacity, column_width), jnp.bfloat16...]
  transfers between devices with their start and end apart: 4 -> 2, of which waited for: 2 -> 0; matrix products, arithmetic and copies ran while one was open for 9% -> 15% of each run, Pallas kernels for 0% -> 0%
where the time goes in v1:
time: 121 us
  Pallas kernels  80.9 us (67%)
  local copies, waits for them, and re-layouts  17.4 us (14%)
  starting transfers between devices  6.83 us (6%)
  other arithmetic  5.42 us (4%)
  blocking collectives  4.03 us (3%)
  matrix products  3.9 us (3%)
  between operations  2.08 us (2%)
    pallas_call x1, Pallas kernels, body(): pl.pallas_call(functools.partial(layer_kernel, count, cap), out_shape=(ja...  80.9 us
    unnamed x6, local copies, waits for them, and re-layouts  15.2 us
    ppermute x2, starting transfers between devices, shifted(): return lax.ppermute(value, axis, pairs)  6.83 us
  transfers between devices with their start and end apart: 2, of which 0 were waited for; matrix products, arithmetic and copies ran while one was open for 15% of the time, Pallas kernels for 0%

profile of v1, /device:TPU:8, one launch (start us, length us, event | category | flops | bytes accessed | tf_op | source)
XLA Modules:
  0.0 120.6 jit_solution(11622571903569531024)
XLA Ops:
  0.6 0.9 copy.20
  1.5 2.0 %all_gather.7 = bf16[256,128]{0,1:T(8,128)(2,1)} all-gather(bf16[128,128]{0,1:T(8,128)(2,1)S(1)} %copy.20), channel_id=1, replica_groups=mesh['ctx'=8,'grp'=2,'head'=2] {'grp'}, dimensions={0}, use_global_device_ids=true | all-gather | bytes 98304 | tf_op jit(solution)/shard_map/all_gather | solution.py:295
  3.5 3.4 %collective-permute-start.1 = (bf16[256,128]{0,1:T(8,128)(2,1)}, bf16[256,128]{0,1:T(8,128)(2,1)S(1)}, u32[]{:S(2)}, u32[]{:S(2)}) collective-permute-start(bf16[256,128]{0,1:T(8,128)(2,1)} %all_gather.7), channel_id=1, source_target_pairs={{0,4},{4,8},{8,12},{12,16},{16,20},{20,24},{24,28},{1,5},{5,9},{9,... | collective-permute-start | bytes 196616 | tf_op jit(solution)/shard_map/while/body/eval_jaxpr/ppermute | solution.py:17
  6.9 0.9 copy.18
  7.8 2.0 %all_gather.6 = bf16[256,128]{0,1:T(8,128)(2,1)} all-gather(bf16[128,128]{0,1:T(8,128)(2,1)S(1)} %copy.18), channel_id=1, replica_groups=mesh['ctx'=8,'grp'=2,'head'=2] {'grp'}, dimensions={0}, use_global_device_ids=true | all-gather | bytes 98304 | tf_op jit(solution)/shard_map/all_gather | solution.py:294
  9.8 3.4 %collective-permute-start = (bf16[256,128]{0,1:T(8,128)(2,1)}, bf16[256,128]{0,1:T(8,128)(2,1)S(1)}, u32[]{:S(2)}, u32[]{:S(2)}) collective-permute-start(bf16[256,128]{0,1:T(8,128)(2,1)} %all_gather.6), channel_id=1, source_target_pairs={{0,4},{4,8},{8,12},{12,16},{16,20},{20,24},{24,28},{1,5},{5,9},{9,... | collective-permute-start | bytes 196616 | tf_op jit(solution)/shard_map/while/body/eval_jaxpr/ppermute | solution.py:17
  13.3 0.9 fusion.27
  14.2 1.4 %reshape.64.gain_ref = f32[2,1440]{1,0:T(2,128)} reshape(f32[2880]{0:T(1024)} %param.17) | data formatting | bytes 23040 | tf_op jit(solution)/shard_map/reshape | solution.py:373
  16.9 1.1 copy.19
  18.1 8.5 %copy.28 = bf16[360,8,2,768]{3,1,2,0:T(8,128)(2,1)} copy(bf16[360,8,2,768]{3,2,1,0:T(2,128)(2,1)} %bitcast.61) | data formatting | bytes 17694720
  26.6 5.3 %conditional.2 = (f32[2,8,128]{2,1,0:T(8,128)}, f32[2,8,128]{2,1,0:T(8,128)S(1)}, f32[2,8,128,64]{2,3,1,0:T(8,128)S(1)}) conditional(s32[]{:T(128)} %convert_element_type.22, () %tuple.30, (pred[128,256]{0,1:T(8,128)(4,1)S(1)}, bf16[256,128]{0,1:T(8,128)(2,1)}, bf16[128,2,8,64]{0,3,2,1:T(8,128)(2,1)S(1)}, bf16[256,128]{0,1:T(8,128)(2,1)}) %tuple.52), branch_computations={%region_2.3_spmd, %region_3.6_spmd} | conditional | flops 141172736 | bytes 7397400 | solution.py:48
  26.6 1.3 %fusion = (f32[2,8,128]{2,1,0:T(8,128)S(1)}, f32[2,256,128,8]{2,1,3,0:T(8,128)S(1)}) fusion(pred[128,256]{0,1:T(8,128)(4,1)S(1)} %get-tuple-element.76, bf16[256,2,64,1]{0,2,3,1:T(8,128)(2,1)} %bitcast.2, bf16[128,2,8,64]{0,3,2,1:T(8,128)(2,1)S(1)} %get-tuple-element.78), kind=kOutput, calls=%fused_computation.2 | convolution fusion | flops 68679680 | bytes 2465792 | tf_op jit(solution)/shard_map/cond/branch_1_fun/tkgd,skd->kgts/dot_general | solution.py:29
  27.9 0.6 exponential_multiply_fusion
  28.5 1.2 fusion.2
  29.7 1.4 %convolution_add_fusion = f32[2,8,128,64]{2,3,1,0:T(8,128)S(1)} fusion(bf16[256,2,64,1]{0,2,3,1:T(8,128)(2,1)} %bitcast.6, f32[2,256,128,8]{2,1,3,0:T(8,128)S(1)} %get-tuple-element.110, f32[2,8,128]{2,1,0:T(8,128)} %get-tuple-element.122, pred[128,256]{0,1:T(8,128)(4,1)S(1)} %get-tuple-element.76, f32[2,8,128]{2,1,0:T(8,128)S(1)} %get-tuple-element.105), kind=kOutput, calls=%fused_computation.5 | convolution fusion | flops 69861376 | bytes 2736128 | tf_op jit(solution)/shard_map/cond/branch_1_fun/kgts,skd->kgtd/dot_general | solution.py:37
  31.1 0.7 fusion.11
  31.9 3.1 %conditional.3 = ((f32[2,8,128]{2,1,0:T(8,128)S(1)}, f32[2,8,128,64]{2,3,1,0:T(8,128)S(1)})) conditional(s32[]{:T(128)} %convert_element_type.21, (f32[2,8,128]{2,1,0:T(8,128)S(1)}, f32[2,8,128,64]{2,3,1,0:T(8,128)S(1)}) %tuple.32, (pred[128,256]{0,1:T(8,128)(4,1)S(1)}, bf16[256,128]{0,1:T(8,128)(2,1)S(1)}, bf16[128,2,8,64]{0,3,2,1:T(8,128)(2,1)S(1)}, ...), branch_computations={%region_6.0_spmd, %region_7.10_spmd} | conditional | flops 141299712 | bytes 7946264 | solution.py:48
  32.4 0.7 max.3
  33.6 0.7 multiply_add_fusion
  34.3 0.7 convolution_add_fusion.1
  35.0 0.9 copy.21.att_ref
  35.9 80.9 %shard_map.95 = (bf16[1440,128]{1,0:T(8,128)(2,1)}, bf16[8,72,768]{2,1,0:T(8,128)(2,1)}) custom-call(bf16[128,1024]{1,0:T(8,128)(2,1)} %copy.21.att_ref, bf16[2880,128]{1,0:T(8,128)(2,1)} %bitcast.67, s32[4,128]{1,0:T(4,128)} %bitcast.70, f32[2,1440]{1,0:T(2,128)} %reshape.64.gain_ref, bf16[2880,1024]{1,0:T(8,128)(2,1)} %bitcast.62, bf16[2880,1536]{1,0:T(8,128)(2,1)} %bitcast.60), custom_call_target="tpu_custom_call" | custom-call | tf_op jit(solution)/shard_map/pallas_call | solution.py:340
  116.8 1.7 %copy.41 = bf16[128,1440]{0,1:T(8,128)(2,1)} copy(bf16[128,1440]{0,1:T(8,128)(2,1)} %bitcast.68) | data formatting | bytes 737280
  118.5 2.1 %copy.42 = bf16[1,1,576,768]{3,2,1,0:T(8,128)(2,1)} copy(bf16[1,1,576,768]{3,2,1,0:T(8,128)(2,1)} %bitcast.66) | data formatting | bytes 1769472
  (8 shorter events, 1.1 us)
Async XLA Ops:
  3.5 28.3 %collective-permute-start.1 = (bf16[256,128]{0,1:T(8,128)(2,1)}, bf16[256,128]{0,1:T(8,128)(2,1)S(1)}, u32[]{:S(2)}, u32[]{:S(2)}) collective-permute-start(bf16[256,128]{0,1:T(8,128)(2,1)} %all_gather.7), channel_id=1, source_target_pairs={{0,4},{4,8},{8,12},{12,16},{16,20},{20,24},{24,28},{1,5},{5,9},{9,... | collective-permute-start | bytes 196616 | tf_op jit(solution)/shard_map/while/body/eval_jaxpr/ppermute | solution.py:17
  9.8 22.0 %collective-permute-start = (bf16[256,128]{0,1:T(8,128)(2,1)}, bf16[256,128]{0,1:T(8,128)(2,1)S(1)}, u32[]{:S(2)}, u32[]{:S(2)}) collective-permute-start(bf16[256,128]{0,1:T(8,128)(2,1)} %all_gather.6), channel_id=1, source_target_pairs={{0,4},{4,8},{8,12},{12,16},{16,20},{20,24},{24,28},{1,5},{5,9},{9,... | collective-permute-start | bytes 196616 | tf_op jit(solution)/shard_map/while/body/eval_jaxpr/ppermute | solution.py:17

commit v2 on v1

--- a/solution.py
+++ b/solution.py
@@ -11,43 +11,6 @@
 TOP = 4
 
 
-def shifted(value, axis, by):
-    count = lax.axis_size(axis)
-    pairs = [(i, i + by) for i in range(count) if 0 <= i + by < count]
-    return lax.ppermute(value, axis, pairs)
-
-
-def attend_block(running, query_heads, key_block, value_block, query_place, key_place, band):
-    allowed = (
-        (key_place[None, :] <= query_place[:, None])
-        & (query_place[:, None] - key_place[None, :] < band)
-        & (key_place[None, :] >= 0)
-    )
-
-    def attend_live(carried):
-        row_max, row_total, summed = carried
-        scores = jnp.einsum(
-            "tkgd,skd->kgts", query_heads, key_block, preferred_element_type=jnp.float32
-        )
-        scores = jnp.where(allowed, scores * query_heads.shape[-1] ** (-0.5), -1e30)
-        new_max = jnp.maximum(row_max, jnp.max(scores, axis=-1))
-        weights = jnp.where(allowed, jnp.exp(scores - new_max[..., None]), 0.0)
-        factor = jnp.exp(row_max - new_max)
-        row_total = row_total * factor + jnp.sum(weights, axis=-1)
-        summed = summed * factor[..., None] + jnp.einsum(
-            "kgts,skd->kgtd",
-            weights.astype(jnp.bfloat16),
-            value_block,
-            preferred_element_type=jnp.float32,
-        )
-        return (new_max, row_total, summed)
-
-    def skip_block(carried):
-        return carried
-
-    return lax.cond(jnp.any(allowed), attend_live, skip_block, running)
-
-
 MESH = pl.DeviceIdType.MESH
 F32 = jnp.float32
 BF16 = jnp.bfloat16
@@ -57,10 +20,72 @@
     return 1 + lax.rem(step + count // 2 - 1, count - 1)
 
 
+def in_pair(values, group, lanes):
+    zeros = jnp.zeros((values.shape[0], HD), values.dtype)
+    if values.shape[1] == HD:
+        return jnp.concatenate([values, zeros], 1), jnp.concatenate([zeros, values], 1)
+    first = group % 2 == 0
+    base = group // 2 * 2 * HD
+    pair = values[:, base : base + 2 * HD]
+    swapped = jnp.concatenate([pair[:, HD:], pair[:, :HD]], 1)
+    low = jnp.where(lanes < HD, pair if first else swapped, jnp.zeros_like(pair))
+    high = jnp.where(lanes >= HD, swapped if first else pair, jnp.zeros_like(pair))
+    return low, high
+
+
+def attend(block, reach, q_ref, kbuf, vbuf, att_ref):
+    tokens = q_ref.shape[0]
+    window = kbuf.shape[0]
+    kv_local = kbuf.shape[1] // HD
+    pairs = q_ref.shape[1] // (2 * HD * kv_local)
+    rows = pairs * tokens
+    place = lax.rem(lax.broadcasted_iota(jnp.int32, (rows, window), 0), tokens)
+    column = lax.broadcasted_iota(jnp.int32, (rows, window), 1)
+    ahead = place + reach * tokens - column
+    allowed = (ahead >= 0) & (ahead < reach * tokens) & (column >= (reach - block) * tokens)
+    lanes = lax.broadcasted_iota(jnp.int32, (window, 2 * HD), 1)
+    left = lax.broadcasted_iota(jnp.int32, (rows, 2 * HD), 1) < HD
+    for group in range(kv_local):
+        key_pair = in_pair(kbuf[...], group, lanes)
+        value_pair = in_pair(vbuf[...], group, lanes)
+        first = group * pairs
+        queries = jnp.concatenate(
+            [
+                q_ref[:, (first + p) * 2 * HD : (first + p + 1) * 2 * HD]
+                for p in range(pairs)
+            ],
+            0,
+        )
+        mixed = jnp.zeros((rows, 2 * HD), F32)
+        totals = []
+        for side in range(2):
+            scores = lax.dot_general(
+                queries,
+                key_pair[side],
+                (((1,), (1,)), ((), ())),
+                preferred_element_type=F32,
+            )
+            scores = jnp.where(allowed, scores * HD ** (-0.5), -1e30)
+            row_max = jnp.max(scores, axis=1, keepdims=True)
+            weights = jnp.where(allowed, jnp.exp(scores - row_max), 0.0)
+            totals.append(jnp.sum(weights, axis=1, keepdims=True))
+            mixed = mixed + jnp.dot(
+                weights.astype(BF16), value_pair[side], preferred_element_type=F32
+            )
+        attended = (mixed / jnp.where(left, totals[0], totals[1])).astype(BF16)
+        for p in range(pairs):
+            att_ref[:, (first + p) * 2 * HD : (first + p + 1) * 2 * HD] = attended[
+                p * tokens : (p + 1) * tokens
+            ]
+
+
 def layer_kernel(
     count,
     cap,
-    att_ref,
+    reach,
+    q_ref,
+    k_ref,
+    v_ref,
     res_ref,
     routes_ref,
     gain_ref,
@@ -68,6 +93,9 @@
     w_hbm,
     hid_ref,
     act_ref,
+    kbuf,
+    vbuf,
+    att_ref,
     ow,
     w,
     psend,
@@ -76,6 +104,8 @@
     before_ref,
     sbuf,
     rbuf,
+    ksend_sem,
+    krecv_sem,
     ow_sem,
     w_sem,
     psend_sem,
@@ -112,6 +142,43 @@
 
     lax.fori_loop(1, count, greet, 0)
 
+    groups = lax.axis_size("grp")
+    block = me * groups + lax.axis_index("grp")
+    blocks = count * groups
+
+    def at_block(index):
+        return {"ctx": index // groups, "grp": lax.rem(index, groups)}
+
+    for j in range(1, reach + 1):
+        for peer in (lax.rem(block + j, blocks), lax.rem(block + blocks - j, blocks)):
+            pl.semaphore_signal(barrier, inc=1, device_id=at_block(peer), device_id_type=MESH)
+
+    def window_copies(j):
+        place = pl.ds((reach - j) * tokens, tokens)
+        target = at_block(lax.rem(block + j, blocks))
+        return [
+            pltpu.make_async_remote_copy(
+                src_ref=source,
+                dst_ref=buffer.at[place],
+                send_sem=ksend_sem.at[n, j - 1],
+                recv_sem=krecv_sem.at[n, j - 1],
+                device_id=target,
+                device_id_type=MESH,
+            )
+            for n, (source, buffer) in enumerate(((k_ref, kbuf), (v_ref, vbuf)))
+        ]
+
+    pl.semaphore_wait(barrier, count - 1 + heads - 1 + 2 * reach)
+    for j in range(1, reach + 1):
+
+        @pl.when(block + j < blocks)
+        def _(j=j):
+            for copy in window_copies(j):
+                copy.start()
+
+    kbuf[reach * tokens :, :] = k_ref[...]
+    vbuf[reach * tokens :, :] = v_ref[...]
+
     def project(slot):
         return lax.dot_general(
             ow[slot], att_ref[...], (((1,), (1,)), ((), ())), preferred_element_type=F32
@@ -127,11 +194,29 @@
             device_id_type=MESH,
         )
 
+    for j in range(1, reach + 1):
+
+        @pl.when(block >= j)
+        def _(j=j):
+            for copy in window_copies(j):
+                copy.wait_recv()
+
+        @pl.when(block < j)
+        def _(j=j):
+            place = pl.ds((reach - j) * tokens, tokens)
+            kbuf[place, :] = jnp.zeros((tokens, kbuf.shape[1]), BF16)
+            vbuf[place, :] = jnp.zeros((tokens, vbuf.shape[1]), BF16)
+
+        @pl.when(block + j < blocks)
+        def _(j=j):
+            for copy in window_copies(j):
+                copy.wait_send()
+
+    attend(block, reach, q_ref, kbuf, vbuf, att_ref)
+
     for j in range(1, heads):
         ow_copy(others[j - 1], j).wait()
         psend[j - 1] = project(j)
-        if j == 1:
-            pl.semaphore_wait(barrier, count - 1 + heads - 1)
         exchange(j).start()
     ow_copy(head, 0).wait()
     projected = project(0).astype(F32)
@@ -277,57 +362,8 @@
 
 def body(residual, queries, keys, values, out_weight, norm_gain, routes, expert_weight):
     tokens_here = queries.shape[0]
-    kv_local = keys.shape[1] // HD
-    per_group = queries.shape[1] // keys.shape[1]
-    query_heads = queries.reshape(tokens_here, kv_local, per_group, HD)
-    ctx_index = lax.axis_index("ctx")
-    grp_index = lax.axis_index("grp")
-    head_index = lax.axis_index("head")
     heads_count = lax.axis_size("head")
-    block_len = tokens_here * lax.axis_size("grp")
-    reach_steps = max(1, lax.axis_size("ctx") // 16)
-    band = reach_steps * block_len
-    query_place = (
-        ctx_index * block_len + grp_index * tokens_here + jnp.arange(tokens_here, dtype=jnp.int32)
-    )
-    own_keys, own_values = (
-        lax.all_gather(keys, "grp", axis=0, tiled=True),
-        lax.all_gather(values, "grp", axis=0, tiled=True),
-    )
-
-    def attend_from(running, key_flat, value_flat, distance):
-        key_place = (ctx_index - distance) * block_len + jnp.arange(block_len, dtype=jnp.int32)
-        return attend_block(
-            running,
-            query_heads,
-            key_flat.reshape(block_len, kv_local, HD),
-            value_flat.reshape(block_len, kv_local, HD),
-            query_place,
-            key_place,
-            band,
-        )
-
-    running = (
-        jnp.full((kv_local, per_group, tokens_here), -1e30, jnp.float32),
-        jnp.zeros((kv_local, per_group, tokens_here), jnp.float32),
-        jnp.zeros((kv_local, per_group, tokens_here, HD), jnp.float32),
-    )
-    running = attend_from(running, own_keys, own_values, 0)
-
-    def cycle_turn(distance, carried):
-        running, key_flat, value_flat = carried
-        key_flat, value_flat = shifted((key_flat, value_flat), "ctx", 1)
-        running = attend_from(running, key_flat, value_flat, distance)
-        return (running, key_flat, value_flat)
-
-    running = lax.fori_loop(1, reach_steps + 1, cycle_turn, (running, own_keys, own_values))[0]
-    row_max, row_total, summed = running
-    mixed = summed / row_total[..., None]
-    attended = (
-        jnp.transpose(mixed, (2, 0, 1, 3))
-        .reshape(tokens_here, kv_local * per_group * HD)
-        .astype(jnp.bfloat16)
-    )
+    reach = max(1, lax.axis_size("ctx") // 16) * lax.axis_size("grp")
     width_all = residual.shape[1]
     half = width_all // heads_count
     count = lax.axis_size("ctx")
@@ -338,14 +374,17 @@
     in_vmem = pl.BlockSpec(memory_space=pltpu.VMEM)
     in_hbm = pl.BlockSpec(memory_space=pl.ANY)
     hidden, active = pl.pallas_call(
-        functools.partial(layer_kernel, count, cap),
+        functools.partial(layer_kernel, count, cap, reach),
         out_shape=(
             jax.ShapeDtypeStruct((half, tokens_here), BF16),
             jax.ShapeDtypeStruct((count, cap, hidden_width), BF16),
         ),
-        in_specs=[in_vmem] * 4 + [in_hbm] * 2,
+        in_specs=[in_vmem] * 6 + [in_hbm] * 2,
         out_specs=(in_vmem, in_vmem),
         scratch_shapes=[
+            pltpu.VMEM(((reach + 1) * tokens_here, keys.shape[1]), BF16),
+            pltpu.VMEM(((reach + 1) * tokens_here, values.shape[1]), BF16),
+            pltpu.VMEM(queries.shape, BF16),
             pltpu.VMEM((heads_count, half, out_weight.shape[0]), BF16),
             pltpu.VMEM((width_all, 2 * hidden_width), BF16),
             pltpu.VMEM((heads_count - 1, half, tokens_here), BF16),
@@ -354,6 +393,8 @@
             pltpu.VMEM((count, tokens_here), F32),
             pltpu.VMEM((count, cap, half), BF16),
             pltpu.VMEM((heads_count, count, cap, half), BF16),
+            pltpu.SemaphoreType.DMA((2, reach)),
+            pltpu.SemaphoreType.DMA((2, reach)),
             pltpu.SemaphoreType.DMA((heads_count,)),
             pltpu.SemaphoreType.DMA,
             pltpu.SemaphoreType.DMA((heads_count - 1,)),
@@ -367,7 +408,9 @@
             collective_id=0, has_side_effects=True, vmem_limit_bytes=60 * 1024 * 1024
         ),
     )(
-        attended,
+        queries,
+        keys,
+        values,
         residual.T,
         routes.T,
         norm_gain.reshape(heads_count, half),

time: 121 us -> 99 us (0.82)
  starting transfers between devices: 6.83 us -> 0 us
  other arithmetic: 5.42 us -> 0 us
  blocking collectives: 4.03 us -> 0 us
  matrix products: 3.9 us -> 0 us
  local copies, waits for them, and re-layouts: 17.4 us -> 13.8 us
  Pallas kernels: 80.9 us -> 84.3 us
  between operations: 2.08 us -> 0.64 us
    ppermute x2 -> x0, starting transfers between devices: 6.83 us -> none  [shifted(): return lax.ppermute(value, axis, pairs)]
    all_gather x2 -> x0, blocking collectives: 4.03 us -> none  [the longest x1 2.02 us: body(): lax.all_gather(keys, 'grp', axis=0, tiled=True)]
    dot_general x4 -> x0, matrix products: 3.9 us -> none  [the longest x2 2.1 us: attend_live(): jnp.einsum('kgts,skd->kgtd', weights.astype(jnp.bfloat16), value_block, p...]
    pallas_call x1, Pallas kernels: 80.9 us -> 84.3 us  [body(): pl.pallas_call(functools.partial(layer_kernel, count, cap, reach), out_sh...]
    unnamed x6 -> x3, local copies, waits for them, and re-layouts: 15.2 us -> 12.4 us
    reduce_sum x2 -> x0, other arithmetic: 1.71 us -> none  [attend_live(): row_total = row_total * factor + jnp.sum(weights, axis=-1)]
    add x4 -> x0, other arithmetic: 1.42 us -> none  [the longest x2 1.42 us: attend_live(): row_total = row_total * factor + jnp.sum(weights, axis=-1)]
  transfers between devices with their start and end apart: 2 -> 0, of which waited for: 0 -> 0; matrix products, arithmetic and copies ran while one was open for 15% -> 0% of each run, Pallas kernels for 0% -> 0%
where the time goes in v2:
time: 99 us; the launch traced here: 98.7 us
  Pallas kernels  84.3 us (85%)
  local copies, waits for them, and re-layouts  13.8 us (14%)
    pallas_call x1, Pallas kernels, body(): pl.pallas_call(functools.partial(layer_kernel, count, cap, reach), out_sh...  84.3 us
    unnamed x3, local copies, waits for them, and re-layouts  12.4 us

profile of v2, /device:TPU:8, one launch (start us, length us, event | category | flops | bytes accessed | tf_op | source)
XLA Modules:
  0.0 98.7 jit_solution(10422523544090895187)
XLA Ops:
  0.6 1.4 %reshape.10.gain_ref = f32[2,1440]{1,0:T(2,128)} reshape(f32[2880]{0:T(1024)} %param.13) | data formatting | bytes 23040 | tf_op jit(solution)/shard_map/reshape | solution.py:416
  2.0 8.5 %copy.10 = bf16[360,8,2,768]{3,1,2,0:T(8,128)(2,1)} copy(bf16[360,8,2,768]{3,2,1,0:T(2,128)(2,1)} %bitcast.9) | data formatting | bytes 17694720
  10.5 84.3 %shard_map.95 = (bf16[1440,128]{1,0:T(8,128)(2,1)}, bf16[8,72,768]{2,1,0:T(8,128)(2,1)}) custom-call(bf16[128,1024]{1,0:T(8,128)(2,1)} %q_ref.1, bf16[128,128]{1,0:T(8,128)(2,1)} %k_ref.1, bf16[128,128]{1,0:T(8,128)(2,1)} %v_ref.1, bf16[2880,128]{1,0:T(8,128)(2,1)} %bitcast.12, s32[4,128]{1,0:T(4,128)} %bitcast.14, f32[2,1440]{1,0:T(2,128)} %reshape.10.gain_ref, ...), custom_call_target="tpu_custom_call" | custom-call | tf_op jit(solution)/shard_map/pallas_call | solution.py:376
  94.8 1.7 %copy.13 = bf16[128,1440]{0,1:T(8,128)(2,1)} copy(bf16[128,1440]{0,1:T(8,128)(2,1)} %bitcast.13) | data formatting | bytes 737280
  96.5 2.1 %copy.14 = bf16[1,1,576,768]{3,2,1,0:T(8,128)(2,1)} copy(bf16[1,1,576,768]{3,2,1,0:T(8,128)(2,1)} %bitcast.11) | data formatting | bytes 1769472

commit v3 on v2

--- a/solution.py
+++ b/solution.py
@@ -97,6 +97,7 @@
     vbuf,
     att_ref,
     ow,
+    paired,
     w,
     psend,
     precv,
@@ -129,7 +130,7 @@
     for j in range(1, heads):
         ow_copy(others[j - 1], j).start()
     ow_copy(head, 0).start()
-    pltpu.make_async_copy(w_hbm, w, w_sem).start()
+    pltpu.make_async_copy(w_hbm, paired, w_sem).start()
 
     barrier = pltpu.get_barrier_semaphore()
     for other in others:
@@ -308,7 +309,16 @@
     lax.fori_loop(0, count - 1, dispatch, 0)
     rbuf[head, me] = rows_for(me)
     cross(me)
-    pltpu.make_async_copy(w_hbm, w, w_sem).wait()
+    pltpu.make_async_copy(w_hbm, paired, w_sem).wait()
+
+    def unpair(step, carry):
+        rows = pl.ds(pl.multiple_of(step * 32, 32), 32)
+        pair = paired[rows]
+        w[rows, :width] = pair[:, 0, :]
+        w[rows, width:] = pair[:, 1, :]
+        return carry
+
+    lax.fori_loop(0, w.shape[0] // 32, unpair, 0)
 
     def expert(source):
         squares = jnp.zeros((cap, 1), F32)
@@ -386,6 +396,7 @@
             pltpu.VMEM(((reach + 1) * tokens_here, values.shape[1]), BF16),
             pltpu.VMEM(queries.shape, BF16),
             pltpu.VMEM((heads_count, half, out_weight.shape[0]), BF16),
+            pltpu.VMEM((width_all, 2, hidden_width), BF16),
             pltpu.VMEM((width_all, 2 * hidden_width), BF16),
             pltpu.VMEM((heads_count - 1, half, tokens_here), BF16),
             pltpu.VMEM((heads_count - 1, half, tokens_here), BF16),
@@ -415,7 +426,7 @@
         routes.T,
         norm_gain.reshape(heads_count, half),
         out_weight.T,
-        expert_weight[0].reshape(width_all, 2 * hidden_width),
+        expert_weight[0],
     )
     return (hidden.T, active.reshape(1, 1, count * cap, hidden_width))
 

time: 99 us -> 90.4 us (0.913)
  local copies, waits for them, and re-layouts: 13.8 us -> 5.27 us
    unnamed x3 -> x2, local copies, waits for them, and re-layouts: 12.4 us -> 3.88 us
where the time goes in v3:
time: 90.4 us; the launch traced here: 90.1 us
  Pallas kernels  84.2 us (93%)
  local copies, waits for them, and re-layouts  5.27 us (6%)
    pallas_call x1, Pallas kernels, body(): pl.pallas_call(functools.partial(layer_kernel, count, cap, reach), out_sh...  84.2 us
    unnamed x2, local copies, waits for them, and re-layouts  3.88 us

profile of v3, /device:TPU:8, one launch (start us, length us, event | category | flops | bytes accessed | tf_op | source)
XLA Modules:
  0.0 90.1 jit_solution(14916469312127888489)
XLA Ops:
  0.6 1.4 %reshape.10.gain_ref = f32[2,1440]{1,0:T(2,128)} reshape(f32[2880]{0:T(1024)} %param.13) | data formatting | bytes 23040 | tf_op jit(solution)/shard_map/reshape | solution.py:427
  2.0 84.2 %shard_map.95 = (bf16[1440,128]{1,0:T(8,128)(2,1)}, bf16[8,72,768]{2,1,0:T(8,128)(2,1)}) custom-call(bf16[128,1024]{1,0:T(8,128)(2,1)} %q_ref.1, bf16[128,128]{1,0:T(8,128)(2,1)} %k_ref.1, bf16[128,128]{1,0:T(8,128)(2,1)} %v_ref.1, bf16[2880,128]{1,0:T(8,128)(2,1)} %bitcast.9, s32[4,128]{1,0:T(4,128)} %bitcast.11, f32[2,1440]{1,0:T(2,128)} %reshape.10.gain_ref, ...), custom_call_target="tpu_custom_call" | custom-call | tf_op jit(solution)/shard_map/pallas_call | solution.py:386
  86.2 1.7 %copy.12 = bf16[128,1440]{0,1:T(8,128)(2,1)} copy(bf16[128,1440]{0,1:T(8,128)(2,1)} %bitcast.10) | data formatting | bytes 737280
  88.0 2.1 %copy.13 = bf16[1,1,576,768]{3,2,1,0:T(8,128)(2,1)} copy(bf16[1,1,576,768]{3,2,1,0:T(8,128)(2,1)} %bitcast.8) | data formatting | bytes 1769472

commit v4 on v3

--- a/solution.py
+++ b/solution.py
@@ -318,7 +318,8 @@
         w[rows, width:] = pair[:, 1, :]
         return carry
 
-    lax.fori_loop(0, w.shape[0] // 32, unpair, 0)
+    pieces = w.shape[0] // 32
+    early = count // 2 - 1
 
     def expert(source):
         squares = jnp.zeros((cap, 1), F32)
@@ -343,21 +344,30 @@
         up = product(width) * inverse_rms
         act_ref[source] = (gate * jax.nn.sigmoid(1.702 * gate) * (up + 1.0)).astype(BF16)
 
-    def receive(step, carry):
+    def source_at(place):
+        turn = turn_of(jnp.maximum(place - 1, 0), count)
+        return jnp.where(place == 0, me, lax.rem(me + count - turn, count))
+
+    def forward(step):
         source = lax.rem(me + count - turn_of(step, count), count)
         landed(source).wait_recv()
         cross(source)
-        before = jnp.where(
-            step == 0, me, lax.rem(me + count - turn_of(jnp.maximum(step - 1, 0), count), count)
-        )
-        mirror(before)
-        expert(before)
-        return carry
-
-    lax.fori_loop(0, count - 1, receive, 0)
-    last = lax.rem(me + count - turn_of(count - 2, count), count)
-    mirror(last)
-    expert(last)
+
+    def receive_early(step, carry):
+        lax.fori_loop(step * pieces // early, (step + 1) * pieces // early, unpair, 0)
+        forward(step)
+        return carry
+
+    def receive(step, carry):
+        forward(step)
+        for side in range(2):
+            source = source_at(2 * (step - early) + side)
+            mirror(source)
+            expert(source)
+        return carry
+
+    lax.fori_loop(0, early, receive_early, 0)
+    lax.fori_loop(early, count - 1, receive, 0)
 
     def drain(step, carry):
         routed(step).wait_send()

time: 90.4 us -> 92.3 us (1.021)
  the two profiles are of different devices: /device:TPU:8 before, /device:TPU:24 now
where the time goes in v4:
time: 92.3 us; the launch traced here: 92 us
  Pallas kernels  86.1 us (93%)
  local copies, waits for them, and re-layouts  5.27 us (6%)
    pallas_call x1, Pallas kernels, body(): pl.pallas_call(functools.partial(layer_kernel, count, cap, reach), out_sh...  86.1 us
    unnamed x2, local copies, waits for them, and re-layouts  3.88 us

profile of v4, /device:TPU:24, one launch (start us, length us, event | category | flops | bytes accessed | tf_op | source)
XLA Modules:
  0.0 92.0 jit_solution(16759718805911285284)
XLA Ops:
  0.6 1.4 %reshape.10.gain_ref = f32[2,1440]{1,0:T(2,128)} reshape(f32[2880]{0:T(1024)} %param.13) | data formatting | bytes 23040 | tf_op jit(solution)/shard_map/reshape | solution.py:437
  2.0 86.1 %shard_map.95 = (bf16[1440,128]{1,0:T(8,128)(2,1)}, bf16[8,72,768]{2,1,0:T(8,128)(2,1)}) custom-call(bf16[128,1024]{1,0:T(8,128)(2,1)} %q_ref.1, bf16[128,128]{1,0:T(8,128)(2,1)} %k_ref.1, bf16[128,128]{1,0:T(8,128)(2,1)} %v_ref.1, bf16[2880,128]{1,0:T(8,128)(2,1)} %bitcast.9, s32[4,128]{1,0:T(4,128)} %bitcast.11, f32[2,1440]{1,0:T(2,128)} %reshape.10.gain_ref, ...), custom_call_target="tpu_custom_call" | custom-call | tf_op jit(solution)/shard_map/pallas_call | solution.py:396
  88.1 1.7 %copy.12 = bf16[128,1440]{0,1:T(8,128)(2,1)} copy(bf16[128,1440]{0,1:T(8,128)(2,1)} %bitcast.10) | data formatting | bytes 737280
  89.8 2.1 %copy.13 = bf16[1,1,576,768]{3,2,1,0:T(8,128)(2,1)} copy(bf16[1,1,576,768]{3,2,1,0:T(8,128)(2,1)} %bitcast.8) | data formatting | bytes 1769472
